TPU v7x, 32 devices: a whole 2x2x4 slice. The times are simulated.
32 devices in a mesh: space: 8 (over z, y), band: 4 (over x, core).
Axes of the slice: x: 2, y: 2, z: 4, core: 2. Of those that a mesh axis runs over, the one named last changes fastest.
Arguments:
- columns: float32 [16, 48, 32, 128], P('band', 'space'), may hold values from -6 to 6
- potential: float32 [48, 32, 128], P('space'), may hold values from -1 to 3
- orbitals: float32 [512, 48, 32, 128], P('band', 'space'), may hold values from -0.0546875 to 0.0546875
Outputs:
- projected: float32 [16, 48, 32, 128], P('band', 'space')
- correlation: float32 [512, 16], P('band')
All inputs are finite; a program needn't handle non-finite values.
Results may differ from a plain program's by a relative error of at most 0.00011.
Values sent between devices are 32-bit elements; how exact they have to be, the bound alone decides.
No kernel may reach another device: no remote copies, remote signals or barrier semaphores. Data moves between devices by JAX's collectives and lax.ppermute only.
A program may use at most 128 MiB of HBM per device.

v0:
```python
import jax
import jax.numpy as jnp
from jax import lax
from jax.sharding import PartitionSpec as P

COEFFS = (
    -5369.0 / 1800.0,
    12.0 / 7.0,
    -15.0 / 56.0,
    10.0 / 189.0,
    -1.0 / 112.0,
    2.0 / 1925.0,
    -1.0 / 16632.0,
)


def padded_2(array, sides, width):
    for axis, dim in sides:
        size, length = (lax.axis_size(axis), array.shape[dim])
        up = [(i, (i + 1) % size) for i in range(size)]
        down = [(j, i) for i, j in up]
        last = lax.slice_in_dim(array, length - width, length, axis=dim)
        first = lax.slice_in_dim(array, 0, width, axis=dim)
        before = lax.ppermute(last, axis, up)
        after = lax.ppermute(first, axis, down)
        array = jnp.concatenate([before, array, after], axis=dim)
    return array


def hamiltonian(values, potential):
    padded = padded_2(values, (("space", 1),), 6)
    planes = values.shape[1]
    laplace = 3.0 * COEFFS[0] * values
    for offset in range(1, 7):
        along = (
            padded[:, 6 + offset : 6 + offset + planes]
            + padded[:, 6 - offset : 6 - offset + planes]
        )
        along = along + jnp.roll(values, offset, 2) + jnp.roll(values, -offset, 2)
        along = along + jnp.roll(values, offset, 3) + jnp.roll(values, -offset, 3)
        laplace = laplace + COEFFS[offset] * along
    return -0.5 * laplace + potential[None] * values


def shards(columns, potential, orbitals):
    applied = hamiltonian(columns, potential)
    orb_local = orbitals.shape[0]
    col_local = applied.shape[0]
    psi_flat = orbitals.reshape(orb_local, -1)
    piece = lax.all_gather(applied, "band", axis=0, tiled=True)
    partial_correlation = jnp.einsum(
        "oc,kc->ok", psi_flat, piece.reshape(piece.shape[0], -1), precision=lax.Precision.HIGHEST
    )
    correlation = lax.psum(partial_correlation, "space")
    removed = jnp.einsum("ok,oc->kc", correlation, psi_flat, precision=lax.Precision.HIGHEST)
    removed_all = lax.psum_scatter(
        removed.reshape((col_local * lax.axis_size("band"),) + applied.shape[1:]),
        "band",
        scatter_dimension=0,
        tiled=True,
    )
    projected = applied - removed_all
    return (projected, correlation)


def solution(mesh):
    placed = (
        P("band", "space", None, None),
        P("space", None, None),
        P("band", "space", None, None),
    )
    return jax.shard_map(
        shards,
        mesh=mesh,
        in_specs=placed,
        out_specs=(P("band", "space", None, None), P("band", None)),
        check_vma=False,
    )
```

profile of v0, /device:TPU:0, one launch (start us, length us, event | category | flops | bytes accessed | tf_op | source)
XLA Modules:
  0.0 155.2 jit_solution(5152359355266835999)
XLA Ops:
  7.2 0.0 copy-start
  7.2 0.0 all-gather.2.cloned.1.call-start
  7.2 3.0 %collective-permute-start.1 = (f32[4,6,32,128]{3,2,1,0:T(8,128)}, f32[4,6,32,128]{3,2,1,0:T(8,128)S(1)}, u32[]{:S(2)}, u32[]{:S(2)}) collective-permute-start(f32[4,6,32,128]{3,2,1,0:T(8,128)} %param.3), channel_id=1, source_target_pairs={{0,4},{4,8},{8,12},{12,16},{16,20},{20,24},{24,28},{28,0},{1,5},{5... | collective-permute-start | bytes 1179656 | tf_op jit(solution)/shard_map/ppermute | solution.py:24
  10.3 3.1 %collective-permute-start = (f32[4,6,32,128]{3,2,1,0:T(8,128)}, f32[4,6,32,128]{3,2,1,0:T(8,128)S(1)}, u32[]{:S(2)}, u32[]{:S(2)}) collective-permute-start(f32[4,6,32,128]{3,2,1,0:T(8,128)} %param.3), channel_id=1, source_target_pairs={{4,0},{8,4},{12,8},{16,12},{20,16},{24,20},{28,24},{0,28},{5,1},{9... | collective-permute-start | bytes 1179656 | tf_op jit(solution)/shard_map/ppermute | solution.py:25
  13.4 1.3 fusion.69
  14.6 1.4 fusion.67
  16.0 1.4 fusion.68
  17.4 1.3 fusion.65
  18.6 1.4 fusion.63
  20.0 0.0 copy-start.2
  20.0 1.4 fusion.64
  21.4 1.3 fusion.61
  22.6 1.0 fusion.62
  23.6 1.4 fusion.59
  25.0 0.0 copy-done
  25.0 0.2 fusion.60
  25.2 0.1 fusion.57
  25.3 0.2 fusion.55
  25.4 0.2 fusion.56
  25.6 0.1 fusion.53
  25.7 0.2 fusion.51
  25.9 0.2 fusion.52
  26.1 0.1 fusion.49
  26.2 0.2 fusion.47
  26.4 0.2 fusion.48
  26.6 0.8 collective-permute-done.1
  27.4 0.1 constant_dynamic-update-slice_fusion.1
  27.5 2.0 %collective-permute-done = f32[4,6,32,128]{3,2,1,0:T(8,128)S(1)} collective-permute-done((f32[4,6,32,128]{3,2,1,0:T(8,128)}, f32[4,6,32,128]{3,2,1,0:T(8,128)S(1)}, u32[]{:S(2)}, u32[]{:S(2)}) %collective-permute-start) | collective-permute-done | bytes 393248 | tf_op jit(solution)/shard_map/ppermute | solution.py:25
  29.5 0.0 copy-done.2
  29.5 3.8 %fusion.16 = f32[4,6,32,128]{3,2,1,0:T(8,128)} fusion(f32[4,12,32,128]{3,2,1,0:T(8,128)S(1)} %get-tuple-element.53, f32[4,12,32,128]{3,2,1,0:T(8,128)S(1)} %constant_dynamic-update-slice_fusion, f32[4,6,31,128]{3,2,1,0:T(8,128)S(1)} %get-tuple-element.49, f32[4,6,1,128]{3,2,1,0:T(1,128)S(1)} %get-tuple-element.51, ...), kind=kLoop, calls=%fused_computation.14 | loop fusion | flops 6881280 | bytes 15040512 | tf_op jit(solution)/shard_map/add | solution.py:42
  33.3 0.0 all-gather.2.cloned.1.call-update
  33.3 0.2 reduce-scatter.2.cloned.1.call-start
  33.6 18.9 %copy.78 = f32[16,8,192,128]{3,1,2,0:T(8,128)} copy(f32[16,8,192,128]{3,2,1,0:T(8,128)} %bitcast.21) | data formatting | bytes 25165824
  52.5 12.6 %copy.64 = f32[24576,128]{1,0:T(8,128)} copy(f32[24576,128]{0,1:T(8,128)} %bitcast.23) | data formatting | bytes 25165824 | tf_op jit(solution)/shard_map/ok,oc->kc/dot_general | solution.py:55
  65.1 0.0 all-gather.2.cloned.1.call-done
  65.1 20.7 %fusion.3 = f32[128,16]{0,1:T(8,128)S(1)} fusion(f32[128,6,32,128]{3,2,1,0:T(8,128)} %param.5, f32[16,6,32,128]{3,2,1,0:T(8,128)} %all-gather.2.cloned.1.call-done), kind=kOutput, calls=%fused_computation.4 | convolution fusion | flops 603979776 | bytes 14163968 | tf_op jit(solution)/shard_map/oc,kc->ok/dot_general | solution.py:51
  85.7 0.0 copy-start.1
  85.8 21.0 %psum.7 = f32[128,16]{0,1:T(8,128)S(1)} all-reduce(f32[128,16]{0,1:T(8,128)S(1)} %fusion.3), channel_id=1, replica_groups=mesh['space'=8,'band'=4] {'space'}, use_global_device_ids=true, to_apply=%region_0.1 | all-reduce | flops 2048 | bytes 16384 | tf_op jit(solution)/shard_map/psum | solution.py:54
  106.7 0.0 copy-start.3
  106.7 12.7 %fusion.45 = f32[16,6,32,128]{3,0,2,1:T(8,128)S(1)} fusion(f32[6,32,128,128]{3,2,1,0:T(8,128)} %bitcast.22, f32[128,16]{0,1:T(8,128)S(1)} %psum.7), kind=kOutput, calls=%fused_computation.52 | convolution fusion | flops 603979776 | bytes 14163968 | tf_op jit(solution)/shard_map/ok,oc->kc/dot_general | solution.py:55
  119.5 1.7 %copy.65 = f32[16,6,32,128]{3,2,1,0:T(8,128)} copy(f32[16,6,32,128]{3,0,2,1:T(8,128)S(1)} %fusion.45) | data formatting | bytes 3145728 | tf_op jit(solution)/shard_map/ok,oc->kc/dot_general | solution.py:55
  121.1 0.0 reduce-scatter.2.cloned.1.call-update
  121.2 25.4 %reduce-scatter.2.cloned.1.call-done = f32[4,6,32,128]{3,2,1,0:T(8,128)} async-done(((f32[16,6,32,128]{3,2,1,0:T(8,128)}), f32[4,6,32,128]{3,2,1,0:T(8,128)}) %reduce-scatter.2.cloned.1.call-update) | async-done | bytes 393232 | tf_op jit(solution)/shard_map/reduce_scatter | solution.py:56
  146.6 0.0 copy-done.1
  146.6 1.8 %sub.3 = f32[4,6,32,128]{3,2,1,0:T(8,128)} subtract(f32[4,6,32,128]{3,2,1,0:T(8,128)S(1)} %copy-done.1, f32[4,6,32,128]{3,2,1,0:T(8,128)} %reduce-scatter.2.cloned.1.call-done) | non-fusion elementwise | flops 98304 | bytes 1179648 | tf_op jit(solution)/shard_map/sub | solution.py:62
  148.4 0.0 copy-done.3
  (7 shorter events, 0.1 us)
Async XLA Ops:
  7.2 17.8 %copy-start = (f32[4,6,32,128]{3,2,1,0:T(8,128)S(1)}, f32[4,6,32,128]{3,2,1,0:T(8,128)}, u32[]{:S(2)}) copy-start(f32[4,6,32,128]{3,2,1,0:T(8,128)} %param.3) | copy-start | bytes 1179652
  7.2 57.9 %all-gather.2.cloned.1.call-start = ((), (), s32[]{:S(2)}) async-start(), calls=%async_computation.1 | async-start | bytes 1966080 | tf_op jit(solution)/shard_map/all_gather | solution.py:50
  7.2 20.2 %collective-permute-start.1 = (f32[4,6,32,128]{3,2,1,0:T(8,128)}, f32[4,6,32,128]{3,2,1,0:T(8,128)S(1)}, u32[]{:S(2)}, u32[]{:S(2)}) collective-permute-start(f32[4,6,32,128]{3,2,1,0:T(8,128)} %param.3), channel_id=1, source_target_pairs={{0,4},{4,8},{8,12},{12,16},{16,20},{20,24},{24,28},{28,0},{1,5},{5... | collective-permute-start | bytes 1179656 | tf_op jit(solution)/shard_map/ppermute | solution.py:24
  10.3 19.2 %collective-permute-start = (f32[4,6,32,128]{3,2,1,0:T(8,128)}, f32[4,6,32,128]{3,2,1,0:T(8,128)S(1)}, u32[]{:S(2)}, u32[]{:S(2)}) collective-permute-start(f32[4,6,32,128]{3,2,1,0:T(8,128)} %param.3), channel_id=1, source_target_pairs={{4,0},{8,4},{12,8},{16,12},{20,16},{24,20},{28,24},{0,28},{5,1},{9... | collective-permute-start | bytes 1179656 | tf_op jit(solution)/shard_map/ppermute | solution.py:25
  20.0 9.5 %copy-start.2 = (f32[6,32,128]{2,1,0:T(8,128)S(1)}, f32[6,32,128]{2,1,0:T(8,128)}, u32[]{:S(2)}) copy-start(f32[6,32,128]{2,1,0:T(8,128)} %param.4) | copy-start | bytes 294916
  33.3 113.2 %reduce-scatter.2.cloned.1.call-start = ((), (), s32[]{:S(2)}) async-start(), calls=%async_computation.2 | async-start | bytes 1966080 | tf_op jit(solution)/shard_map/reduce_scatter | solution.py:56
  85.7 60.8 %copy-start.1 = (f32[4,6,32,128]{3,2,1,0:T(8,128)S(1)}, f32[4,6,32,128]{3,2,1,0:T(8,128)}, u32[]{:S(2)}) copy-start(f32[4,6,32,128]{3,2,1,0:T(8,128)} %fusion.16) | copy-start | bytes 1179652
  106.7 41.6 %copy-start.3 = (f32[128,16]{0,1:T(8,128)}, f32[128,16]{0,1:T(8,128)S(1)}, u32[]{:S(2)}) copy-start(f32[128,16]{0,1:T(8,128)S(1)} %psum.7) | copy-start | bytes 24580
Sparse Core Ops, SparseCore 0:
  33.5 19.7 all-gather.1
  121.3 25.2 reduce-scatter.1
where the time goes:
time: 156 us; the launch traced here: 155 us
  local copies, waits for them, and re-layouts  46.5 us (30%)
  matrix products  33.4 us (21%)
  waiting for transfers between devices  28.2 us (18%)
  blocking collectives  21 us (13%)
  between operations  14.2 us (9%)
  starting transfers between devices  6.41 us (4%)
  other arithmetic  5.59 us (4%)
    reduce_scatter x1, waiting for transfers between devices, shards(): lax.psum_scatter(removed.reshape((col_local * lax.axis_size('band'),) + a...  25.4 us
    psum x1, blocking collectives, shards(): correlation = lax.psum(partial_correlation, 'space')  21 us
    dot_general x1, matrix products, shards(): jnp.einsum('oc,kc->ok', psi_flat, piece.reshape(piece.shape[0], -1), prec...  20.7 us
    unnamed x11, local copies, waits for them, and re-layouts  19 us
    dot_general x2, local copies, waits for them, and re-layouts, shards(): jnp.einsum('ok,oc->kc', correlation, psi_flat, precision=lax.Precision.HI...  14.3 us
    dot_general x1, matrix products, shards(): jnp.einsum('ok,oc->kc', correlation, psi_flat, precision=lax.Precision.HI...  12.7 us
    slice x12, local copies, waits for them, and re-layouts, hamiltonian(): along = along + jnp.roll(values, offset, 3) + jnp.roll(values, -offset, 3)  8.09 us
    slice x12, local copies, waits for them, and re-layouts, hamiltonian(): along = along + jnp.roll(values, offset, 2) + jnp.roll(values, -offset, 2)  5.05 us
  transfers between devices with their start and end apart: 4, of which 3 were waited for; matrix products, arithmetic and copies ran while one was open for 29% of the time, Pallas kernels for 0%

commit v1 on v0

--- a/solution.py
+++ b/solution.py
@@ -51,7 +51,11 @@
     partial_correlation = jnp.einsum(
         "oc,kc->ok", psi_flat, piece.reshape(piece.shape[0], -1), precision=lax.Precision.HIGHEST
     )
-    correlation = lax.psum(partial_correlation, "space")
+    correlation = partial_correlation
+    for hop in (1, 2, 4):
+        correlation = correlation + lax.ppermute(
+            correlation, "space", [(dev, dev ^ hop) for dev in range(8)]
+        )
     removed = jnp.einsum("ok,oc->kc", correlation, psi_flat, precision=lax.Precision.HIGHEST)
     removed_all = lax.psum_scatter(
         removed.reshape((col_local * lax.axis_size("band"),) + applied.shape[1:]),

time: 156 us -> 166 us (1.064)
  waiting for transfers between devices: 28.2 us -> 53.3 us
  blocking collectives: 21 us -> 0 us
  starting transfers between devices: 6.41 us -> 11.7 us
    psum x1 -> x0, blocking collectives: 21 us -> none  [shards(): correlation = lax.psum(partial_correlation, 'space')]
    all_gather x1, waiting for transfers between devices: 0.01 us -> 19.9 us  [shards(): piece = lax.all_gather(applied, 'band', axis=0, tiled=True)]
    ppermute x0 -> x3, starting transfers between devices: none -> 5.43 us  [shards(): lax.ppermute(correlation, 'space', [(dev, dev ^ hop) for dev in range(8)])]
    ppermute x0 -> x3, waiting for transfers between devices: none -> 4.35 us  [shards(): lax.ppermute(correlation, 'space', [(dev, dev ^ hop) for dev in range(8)])]
  transfers between devices with their start and end apart: 4 -> 7, of which waited for: 3 -> 6; matrix products, arithmetic and copies ran while one was open for 29% -> 27% of each run, Pallas kernels for 0% -> 0%
where the time goes in v1:
time: 166 us; the launch traced here: 165 us
  waiting for transfers between devices  53.3 us (32%)
  local copies, waits for them, and re-layouts  46.5 us (28%)
  matrix products  33.7 us (20%)
  between operations  14.2 us (9%)
  starting transfers between devices  11.7 us (7%)
  other arithmetic  5.6 us (3%)
    reduce_scatter x1, waiting for transfers between devices, shards(): lax.psum_scatter(removed.reshape((col_local * lax.axis_size('band'),) + a...  26.4 us
    dot_general x1, matrix products, shards(): jnp.einsum('oc,kc->ok', psi_flat, piece.reshape(piece.shape[0], -1), prec...  20.8 us
    all_gather x1, waiting for transfers between devices, shards(): piece = lax.all_gather(applied, 'band', axis=0, tiled=True)  19.9 us
    unnamed x11, local copies, waits for them, and re-layouts  19 us
    dot_general x2, local copies, waits for them, and re-layouts, shards(): jnp.einsum('ok,oc->kc', correlation, psi_flat, precision=lax.Precision.HI...  14.3 us
    dot_general x1, matrix products, shards(): jnp.einsum('ok,oc->kc', correlation, psi_flat, precision=lax.Precision.HI...  12.9 us
    slice x12, local copies, waits for them, and re-layouts, hamiltonian(): along = along + jnp.roll(values, offset, 3) + jnp.roll(values, -offset, 3)  8.09 us
    ppermute x3, starting transfers between devices, shards(): lax.ppermute(correlation, 'space', [(dev, dev ^ hop) for dev in range(8)])  5.43 us
  transfers between devices with their start and end apart: 7, of which 6 were waited for; matrix products, arithmetic and copies ran while one was open for 27% of the time, Pallas kernels for 0%

profile of v1, /device:TPU:0, one launch (start us, length us, event | category | flops | bytes accessed | tf_op | source)
XLA Modules:
  0.0 165.0 jit_solution(17690337462435963354)
XLA Ops:
  7.2 0.0 copy-start
  7.2 0.0 all-gather.2.cloned.1.call-start
  7.2 3.0 %collective-permute-start.1 = (f32[4,6,32,128]{3,2,1,0:T(8,128)}, f32[4,6,32,128]{3,2,1,0:T(8,128)S(1)}, u32[]{:S(2)}, u32[]{:S(2)}) collective-permute-start(f32[4,6,32,128]{3,2,1,0:T(8,128)} %param.3), channel_id=1, source_target_pairs={{0,4},{4,8},{8,12},{12,16},{16,20},{20,24},{24,28},{28,0},{1,5},{5... | collective-permute-start | bytes 1179656 | tf_op jit(solution)/shard_map/ppermute | solution.py:24
  10.3 3.1 %collective-permute-start = (f32[4,6,32,128]{3,2,1,0:T(8,128)}, f32[4,6,32,128]{3,2,1,0:T(8,128)S(1)}, u32[]{:S(2)}, u32[]{:S(2)}) collective-permute-start(f32[4,6,32,128]{3,2,1,0:T(8,128)} %param.3), channel_id=1, source_target_pairs={{4,0},{8,4},{12,8},{16,12},{20,16},{24,20},{28,24},{0,28},{5,1},{9... | collective-permute-start | bytes 1179656 | tf_op jit(solution)/shard_map/ppermute | solution.py:25
  13.4 1.3 fusion.69
  14.6 1.4 fusion.67
  16.0 1.4 fusion.68
  17.4 1.3 fusion.65
  18.6 1.4 fusion.63
  20.0 0.0 copy-start.2
  20.0 1.4 fusion.64
  21.4 1.3 fusion.61
  22.6 1.0 fusion.62
  23.6 1.4 fusion.59
  25.0 0.0 copy-done
  25.0 0.2 fusion.60
  25.2 0.1 fusion.57
  25.3 0.2 fusion.55
  25.4 0.2 fusion.56
  25.6 0.1 fusion.53
  25.7 0.2 fusion.51
  25.9 0.2 fusion.52
  26.1 0.1 fusion.49
  26.2 0.2 fusion.47
  26.4 0.2 fusion.48
  26.6 0.8 collective-permute-done.1
  27.4 0.1 constant_dynamic-update-slice_fusion.1
  27.5 2.0 %collective-permute-done = f32[4,6,32,128]{3,2,1,0:T(8,128)S(1)} collective-permute-done((f32[4,6,32,128]{3,2,1,0:T(8,128)}, f32[4,6,32,128]{3,2,1,0:T(8,128)S(1)}, u32[]{:S(2)}, u32[]{:S(2)}) %collective-permute-start) | collective-permute-done | bytes 393248 | tf_op jit(solution)/shard_map/ppermute | solution.py:25
  29.5 0.0 copy-done.2
  29.5 3.8 %fusion.16 = f32[4,6,32,128]{3,2,1,0:T(8,128)} fusion(f32[4,12,32,128]{3,2,1,0:T(8,128)S(1)} %get-tuple-element.53, f32[4,12,32,128]{3,2,1,0:T(8,128)S(1)} %constant_dynamic-update-slice_fusion, f32[4,6,31,128]{3,2,1,0:T(8,128)S(1)} %get-tuple-element.49, f32[4,6,1,128]{3,2,1,0:T(1,128)S(1)} %get-tuple-element.51, ...), kind=kLoop, calls=%fused_computation.14 | loop fusion | flops 6881280 | bytes 15040512 | tf_op jit(solution)/shard_map/add | solution.py:42
  33.3 0.0 all-gather.2.cloned.1.call-update
  33.3 0.0 reduce-scatter.2.cloned.1.call-start
  33.4 19.9 %all-gather.2.cloned.1.call-done = f32[16,6,32,128]{3,2,1,0:T(8,128)} async-done(((f32[4,6,32,128]{3,2,1,0:T(8,128)}), f32[16,6,32,128]{3,2,1,0:T(8,128)}) %all-gather.2.cloned.1.call-update) | async-done | bytes 1572880 | tf_op jit(solution)/shard_map/all_gather | solution.py:50
  53.3 20.8 %fusion.3 = f32[128,16]{0,1:T(8,128)S(1)} fusion(f32[128,6,32,128]{3,2,1,0:T(8,128)} %param.5, f32[16,6,32,128]{3,2,1,0:T(8,128)} %all-gather.2.cloned.1.call-done), kind=kOutput, calls=%fused_computation.4 | convolution fusion | flops 603979776 | bytes 14163968 | tf_op jit(solution)/shard_map/oc,kc->ok/dot_general | solution.py:51
  74.0 1.5 collective-permute-start.2
  75.6 2.2 %collective-permute-done.2 = f32[128,16]{0,1:T(8,128)S(1)} collective-permute-done((f32[128,16]{0,1:T(8,128)S(1)}, f32[128,16]{0,1:T(8,128)S(1)}, u32[]{:S(2)}, u32[]{:S(2)}) %collective-permute-start.2) | collective-permute-done | bytes 8224 | tf_op jit(solution)/shard_map/ppermute | solution.py:56
  77.8 1.5 collective-permute-start.3
  79.2 2.2 %collective-permute-done.3 = f32[128,16]{0,1:T(8,128)S(1)} collective-permute-done((f32[128,16]{0,1:T(8,128)S(1)}, f32[128,16]{0,1:T(8,128)S(1)}, u32[]{:S(2)}, u32[]{:S(2)}) %collective-permute-start.3) | collective-permute-done | bytes 8224 | tf_op jit(solution)/shard_map/ppermute | solution.py:56
  81.4 2.4 %collective-permute-start.4 = (f32[128,16]{0,1:T(8,128)S(1)}, f32[128,16]{0,1:T(8,128)S(1)}, u32[]{:S(2)}, u32[]{:S(2)}) collective-permute-start(f32[128,16]{0,1:T(8,128)S(1)} %add.160), channel_id=1, source_target_pairs={{0,16},{4,20},{8,24},{12,28},{16,0},{20,4},{24,8},{28,12},{1,17},{... | collective-permute-start | bytes 24584 | tf_op jit(solution)/shard_map/ppermute | solution.py:56
  83.8 18.9 %copy.78 = f32[16,8,192,128]{3,1,2,0:T(8,128)} copy(f32[16,8,192,128]{3,2,1,0:T(8,128)} %bitcast.21) | data formatting | bytes 25165824
  102.7 12.6 %copy.64 = f32[24576,128]{1,0:T(8,128)} copy(f32[24576,128]{0,1:T(8,128)} %bitcast.23) | data formatting | bytes 25165824 | tf_op jit(solution)/shard_map/ok,oc->kc/dot_general | solution.py:59
  115.4 0.0 copy-start.1
  115.4 0.0 collective-permute-done.4
  115.4 0.0 copy-start.3
  115.4 12.9 %fusion.45 = f32[16,6,32,128]{3,0,2,1:T(8,128)S(1)} fusion(f32[6,32,128,128]{3,2,1,0:T(8,128)} %bitcast.22, f32[128,16]{0,1:T(8,128)S(1)} %add.161), kind=kOutput, calls=%fused_computation.52 | convolution fusion | flops 603979776 | bytes 14163968 | tf_op jit(solution)/shard_map/ok,oc->kc/dot_general | solution.py:59
  128.3 1.7 %copy.65 = f32[16,6,32,128]{3,2,1,0:T(8,128)} copy(f32[16,6,32,128]{3,0,2,1:T(8,128)S(1)} %fusion.45) | data formatting | bytes 3145728 | tf_op jit(solution)/shard_map/ok,oc->kc/dot_general | solution.py:59
  130.0 0.0 reduce-scatter.2.cloned.1.call-update
  130.0 26.4 %reduce-scatter.2.cloned.1.call-done = f32[4,6,32,128]{3,2,1,0:T(8,128)} async-done(((f32[16,6,32,128]{3,2,1,0:T(8,128)}), f32[4,6,32,128]{3,2,1,0:T(8,128)}) %reduce-scatter.2.cloned.1.call-update) | async-done | bytes 393232 | tf_op jit(solution)/shard_map/reduce_scatter | solution.py:60
  156.4 0.0 copy-done.1
  156.4 1.8 %sub.3 = f32[4,6,32,128]{3,2,1,0:T(8,128)} subtract(f32[4,6,32,128]{3,2,1,0:T(8,128)S(1)} %copy-done.1, f32[4,6,32,128]{3,2,1,0:T(8,128)} %reduce-scatter.2.cloned.1.call-done) | non-fusion elementwise | flops 98304 | bytes 1179648 | tf_op jit(solution)/shard_map/sub | solution.py:66
  158.2 0.0 copy-done.3
  (10 shorter events, 0.2 us)
Async XLA Ops:
  7.2 17.8 %copy-start = (f32[4,6,32,128]{3,2,1,0:T(8,128)S(1)}, f32[4,6,32,128]{3,2,1,0:T(8,128)}, u32[]{:S(2)}) copy-start(f32[4,6,32,128]{3,2,1,0:T(8,128)} %param.3) | copy-start | bytes 1179652
  7.2 46.1 %all-gather.2.cloned.1.call-start = ((), (), s32[]{:S(2)}) async-start(), calls=%async_computation.1 | async-start | bytes 1966080 | tf_op jit(solution)/shard_map/all_gather | solution.py:50
  7.2 20.2 %collective-permute-start.1 = (f32[4,6,32,128]{3,2,1,0:T(8,128)}, f32[4,6,32,128]{3,2,1,0:T(8,128)S(1)}, u32[]{:S(2)}, u32[]{:S(2)}) collective-permute-start(f32[4,6,32,128]{3,2,1,0:T(8,128)} %param.3), channel_id=1, source_target_pairs={{0,4},{4,8},{8,12},{12,16},{16,20},{20,24},{24,28},{28,0},{1,5},{5... | collective-permute-start | bytes 1179656 | tf_op jit(solution)/shard_map/ppermute | solution.py:24
  10.3 19.2 %collective-permute-start = (f32[4,6,32,128]{3,2,1,0:T(8,128)}, f32[4,6,32,128]{3,2,1,0:T(8,128)S(1)}, u32[]{:S(2)}, u32[]{:S(2)}) collective-permute-start(f32[4,6,32,128]{3,2,1,0:T(8,128)} %param.3), channel_id=1, source_target_pairs={{4,0},{8,4},{12,8},{16,12},{20,16},{24,20},{28,24},{0,28},{5,1},{9... | collective-permute-start | bytes 1179656 | tf_op jit(solution)/shard_map/ppermute | solution.py:25
  20.0 9.5 %copy-start.2 = (f32[6,32,128]{2,1,0:T(8,128)S(1)}, f32[6,32,128]{2,1,0:T(8,128)}, u32[]{:S(2)}) copy-start(f32[6,32,128]{2,1,0:T(8,128)} %param.4) | copy-start | bytes 294916
  33.3 123.0 %reduce-scatter.2.cloned.1.call-start = ((), (), s32[]{:S(2)}) async-start(), calls=%async_computation.2 | async-start | bytes 1966080 | tf_op jit(solution)/shard_map/reduce_scatter | solution.py:60
  74.0 3.7 %collective-permute-start.2 = (f32[128,16]{0,1:T(8,128)S(1)}, f32[128,16]{0,1:T(8,128)S(1)}, u32[]{:S(2)}, u32[]{:S(2)}) collective-permute-start(f32[128,16]{0,1:T(8,128)S(1)} %fusion.3), channel_id=1, source_target_pairs={{0,4},{4,0},{8,12},{12,8},{16,20},{20,16},{24,28},{28,24},{1,5},{5... | collective-permute-start | bytes 24584 | tf_op jit(solution)/shard_map/ppermute | solution.py:56
  77.8 3.7 %collective-permute-start.3 = (f32[128,16]{0,1:T(8,128)S(1)}, f32[128,16]{0,1:T(8,128)S(1)}, u32[]{:S(2)}, u32[]{:S(2)}) collective-permute-start(f32[128,16]{0,1:T(8,128)S(1)} %add.159), channel_id=1, source_target_pairs={{0,8},{4,12},{8,0},{12,4},{16,24},{20,28},{24,16},{28,20},{1,9},{5... | collective-permute-start | bytes 24584 | tf_op jit(solution)/shard_map/ppermute | solution.py:56
  81.4 33.9 %collective-permute-start.4 = (f32[128,16]{0,1:T(8,128)S(1)}, f32[128,16]{0,1:T(8,128)S(1)}, u32[]{:S(2)}, u32[]{:S(2)}) collective-permute-start(f32[128,16]{0,1:T(8,128)S(1)} %add.160), channel_id=1, source_target_pairs={{0,16},{4,20},{8,24},{12,28},{16,0},{20,4},{24,8},{28,12},{1,17},{... | collective-permute-start | bytes 24584 | tf_op jit(solution)/shard_map/ppermute | solution.py:56
  115.4 41.0 %copy-start.1 = (f32[4,6,32,128]{3,2,1,0:T(8,128)S(1)}, f32[4,6,32,128]{3,2,1,0:T(8,128)}, u32[]{:S(2)}) copy-start(f32[4,6,32,128]{3,2,1,0:T(8,128)} %fusion.16) | copy-start | bytes 1179652
  115.4 42.8 %copy-start.3 = (f32[128,16]{0,1:T(8,128)}, f32[128,16]{0,1:T(8,128)S(1)}, u32[]{:S(2)}) copy-start(f32[128,16]{0,1:T(8,128)S(1)} %add.161) | copy-start | bytes 24580
Sparse Core Ops, SparseCore 0:
  33.5 19.7 all-gather.1
  130.1 26.1 reduce-scatter.1
